TPU v7x, 32 devices: a whole 2x2x4 slice. The times are simulated.
32 devices in a mesh: groups: 2 (over x), dp: 16 (over z, y, core).
Axes of the slice: x: 2, y: 2, z: 4, core: 2. Of those that a mesh axis runs over, the one named last changes fastest.
Arguments:
- inputs: bfloat16 [8192, 4096], P(('groups', 'dp')), parts along dimension 0, may hold values from -6 to 6
- gate_values: bfloat16 [8192, 4096], P(('groups', 'dp')), parts along dimension 0, may hold values from -6 to 6
- write_proj: bfloat16 [8192, 128], P(('groups', 'dp')), parts along dimension 0, may hold values from -6 to 6
- read_proj: bfloat16 [8192, 128], P(('groups', 'dp')), parts along dimension 0, may hold values from -0.59765625 to 0.59765625
- step_raw: bfloat16 [8192, 64], P(('groups', 'dp')), parts along dimension 0, may hold values from -3 to 10
- cotangent: bfloat16 [8192, 4096], P(('groups', 'dp')), parts along dimension 0, may hold values from -6 to 6
- step_bias: float32 [64], replicated, may hold values from -5.5 to -3.5
- rate_log: float32 [64], replicated
- skip_gain: float32 [64], replicated, may hold values from 0.5 to 1.5
- norm_gain: float32 [4096], replicated, may hold values from 0.5 to 1.5
- state_bank: bfloat16 [128, 64, 64, 128], P('groups', 'dp'), parts along dimension 0, may hold values from -1.796875 to 1.796875
- turn_index: int32 [8192], P(('groups', 'dp')), parts along dimension 0, may hold values from 0 to 3, as said below
- turn_slot: int32 [128], P('groups'), parts along dimension 0, may hold values from 0 to 63, each once
Outputs:
- grad_inputs: bfloat16 [8192, 4096], P(('groups', 'dp')), parts along dimension 0
- state_grad: bfloat16 [128, 64, 64, 128], P('groups', 'dp'), parts along dimension 0
- gain_grad: float32 [8192], P(('groups', 'dp')), parts along dimension 0
- head_grads: float32 [6, 64], P('groups'), parts along dimension 0
There are 2 independent parts, one for each index of `groups`. A program takes and returns all parts, laid end to end along the dimension named above; an argument that names none is the same for every part. Nothing has to cross between parts.
Inputs may be any that keep to these rules, and one draw needn't show every extreme that they name: `turn_index`: within each device's 256 tokens turn numbers start at 0, never fall and rise by one at each new turn; some device has 4 turns. `turn_slot`: each slot number appears once.
All inputs are finite; a program needn't handle non-finite values.
Results may differ from a plain program's by a relative error of at most 0.0051.
Values may be sent and summed in bfloat16 or wider, within the bound.
No kernel may reach another device: no remote copies, remote signals or barrier semaphores. Data moves between devices by JAX's collectives and lax.ppermute only.
A program may use at most 128 MiB of HBM per device.

v0:
```python
import jax
import jax.numpy as jnp
from jax import lax
from jax.sharding import PartitionSpec as P

HDIM = 64
DSTATE = 128
BLOCK_LEN = 256
TMAX = 4


def project_turns(states, read_proj, turn_index):
    turn_cap = states.shape[0]
    onehot = turn_index[:, None] == jnp.arange(turn_cap, dtype=jnp.int32)[None, :]
    masked = jnp.where(onehot[:, :, None], read_proj[:, None, :], jnp.zeros((), read_proj.dtype))
    return jnp.einsum("tgn,ghpn->thp", masked, states, preferred_element_type=jnp.float32).astype(
        jnp.bfloat16
    )


def turn_grads(read_grad, read_proj, turn_index, turn_cap):
    onehot = turn_index[:, None] == jnp.arange(turn_cap, dtype=jnp.int32)[None, :]
    masked = jnp.where(onehot[:, :, None], read_proj[:, None, :], jnp.zeros((), read_proj.dtype))
    return jnp.einsum("tgn,thp->ghpn", masked, read_grad, preferred_element_type=jnp.float32)


def mixer(
    input_value,
    start_read,
    bias_value,
    rate_value,
    skip_value,
    gain_value,
    gate_values,
    write_proj,
    read_proj,
    step_raw,
    turn_index,
):
    row_count = input_value.shape[0]
    head_count = step_raw.shape[1]
    head_dim = input_value.shape[1] // head_count
    state_dim = write_proj.shape[1]
    block_count = row_count // BLOCK_LEN
    highest = lax.Precision.HIGHEST
    step_size = jax.nn.softplus(step_raw.astype(jnp.float32) + bias_value[None, :])
    log_decay = -jnp.exp(rate_value)[None, :] * step_size
    starts = jnp.concatenate([jnp.ones((1,), jnp.bool_), turn_index[1:] != turn_index[:-1]])
    blocked = (
        input_value.reshape(block_count, BLOCK_LEN, head_count, head_dim),
        write_proj.reshape(block_count, BLOCK_LEN, state_dim),
        read_proj.reshape(block_count, BLOCK_LEN, state_dim),
        step_size.reshape(block_count, BLOCK_LEN, head_count),
        log_decay.reshape(block_count, BLOCK_LEN, head_count),
        turn_index.reshape(block_count, BLOCK_LEN),
        starts.reshape(block_count, BLOCK_LEN),
        start_read.reshape(block_count, BLOCK_LEN, head_count, head_dim),
    )
    token_positions = jnp.arange(BLOCK_LEN, dtype=jnp.int32)
    causal_mask = token_positions[:, None] >= token_positions[None, :]

    def advance(carried, pieces):
        state_now, since_now = carried
        (
            block_x,
            block_write,
            block_read,
            block_step,
            block_decay,
            block_turn,
            block_start,
            block_begin,
        ) = pieces
        running = jnp.cumsum(block_decay, axis=0)
        before = running - block_decay
        same_mask = (causal_mask & (block_turn[:, None] == block_turn[None, :]))[:, :, None]
        decay_mat = jnp.exp(jnp.where(same_mask, running[:, None, :] - running[None, :, :], -1e30))
        offset = jnp.max(jnp.where(same_mask, before[None, :, :], -1e30), axis=1)
        scores = jnp.dot(block_read, block_write.T, preferred_element_type=jnp.float32)
        weights = decay_mat * scores[:, :, None] * block_step[None, :, :]
        local_part = jnp.einsum("tsh,shp->thp", weights, block_x, precision=highest)
        kept = ((block_turn == block_turn[0]) & jnp.logical_not(block_start[0])).astype(jnp.float32)
        inner = running - offset
        read_f = block_read.astype(jnp.float32)
        projected = jnp.einsum("hpn,tn->thp", state_now, read_f, precision=highest)
        since = inner + kept[:, None] * since_now[None, :]
        carry_factor = jnp.exp(inner) * kept[:, None]
        output = (
            local_part
            + carry_factor[:, :, None] * projected
            + jnp.exp(since)[:, :, None] * block_begin
            + skip_value[None, :, None] * block_x
        )
        last_weights = decay_mat[-1] * block_step
        new_state = carry_factor[-1][:, None, None] * state_now + jnp.einsum(
            "sh,shp,sn->hpn",
            last_weights,
            block_x,
            block_write.astype(jnp.float32),
            precision=highest,
        )
        return ((new_state, since[-1]), output)

    start_state = (
        jnp.zeros((head_count, head_dim, state_dim), jnp.float32),
        jnp.zeros((head_count,), jnp.float32),
    )
    final_state, outputs = lax.scan(advance, start_state, blocked)
    mixed = outputs.reshape(row_count, head_count, head_dim)
    gate_f = gate_values.astype(jnp.float32).reshape(row_count, head_count, head_dim)
    gated_out = mixed * jax.nn.silu(gate_f)
    mean_square = jnp.mean(gated_out * gated_out, axis=-1, keepdims=True)
    normed = (
        gated_out * lax.rsqrt(mean_square + 1e-05) * gain_value.reshape(head_count, head_dim)[None]
    )
    return normed.reshape(row_count, head_count * head_dim)


def learner(
    inputs,
    start_read,
    step_bias,
    rate_log,
    skip_gain,
    norm_gain,
    gate_values,
    write_proj,
    read_proj,
    step_raw,
    turn_index,
    cotangent,
):

    def forward(input_value, read_value, bias_value, rate_value, skip_value, gain_value):
        return mixer(
            input_value,
            read_value,
            bias_value,
            rate_value,
            skip_value,
            gain_value,
            gate_values,
            write_proj,
            read_proj,
            step_raw,
            turn_index,
        )

    primal, pullback = jax.vjp(
        forward,
        inputs.astype(jnp.float32),
        start_read.astype(jnp.float32),
        step_bias,
        rate_log,
        skip_gain,
        norm_gain,
    )
    return pullback(cotangent.astype(jnp.float32))


def local(
    inputs,
    gate_values,
    write_proj,
    read_proj,
    step_raw,
    cotangent,
    step_bias,
    rate_log,
    skip_gain,
    norm_gain,
    state_bank,
    turn_index,
    turn_slot,
):
    devices = lax.axis_size("dp")
    inverse = jnp.argsort(turn_slot)
    head_part = state_bank.shape[1]
    row_count = inputs.shape[0]
    position = lax.axis_index("dp")
    moved_inputs, moved_gates, moved_cot, moved_steps = (
        lax.all_to_all(inputs, "dp", split_axis=1, concat_axis=0, tiled=True),
        lax.all_to_all(gate_values, "dp", split_axis=1, concat_axis=0, tiled=True),
        lax.all_to_all(cotangent, "dp", split_axis=1, concat_axis=0, tiled=True),
        lax.all_to_all(step_raw, "dp", split_axis=1, concat_axis=0, tiled=True),
    )
    write_all, read_all = (
        lax.all_gather(write_proj, "dp", axis=0, tiled=True),
        lax.all_gather(read_proj, "dp", axis=0, tiled=True),
    )
    turns_all = lax.all_gather(turn_index, "dp", axis=0, tiled=True)
    start_head = position * head_part
    own_bias = lax.dynamic_slice_in_dim(step_bias, start_head, head_part)
    own_rate = lax.dynamic_slice_in_dim(rate_log, start_head, head_part)
    own_skip = lax.dynamic_slice_in_dim(skip_gain, start_head, head_part)
    own_gain = lax.dynamic_slice_in_dim(norm_gain, start_head * HDIM, head_part * HDIM)
    initial = state_bank[turn_slot].reshape(devices, TMAX, head_part, HDIM, DSTATE)

    def split_rows(value):
        return value.reshape((devices, row_count) + value.shape[1:])

    read_split = split_rows(read_all)
    turns_split = split_rows(turns_all)
    start_read = jax.vmap(project_turns)(initial, read_split, turns_split)
    batched = jax.vmap(learner, in_axes=(0, 0, None, None, None, None, 0, 0, 0, 0, 0, 0))
    gradients = batched(
        split_rows(moved_inputs),
        start_read,
        own_bias,
        own_rate,
        own_skip,
        own_gain,
        split_rows(moved_gates),
        split_rows(write_all),
        read_split,
        split_rows(moved_steps),
        turns_split,
        split_rows(moved_cot),
    )
    grad_local = gradients[0].reshape(devices * row_count, head_part * HDIM).astype(jnp.bfloat16)
    grad_inputs = lax.all_to_all(grad_local, "dp", split_axis=0, concat_axis=1, tiled=True)
    read_grad = gradients[1].astype(jnp.bfloat16)
    holder_turns = jax.vmap(turn_grads, in_axes=(0, 0, 0, None))(
        read_grad, read_split, turns_split, TMAX
    )
    state_grad = holder_turns.reshape(devices * TMAX, head_part, HDIM, DSTATE).astype(jnp.bfloat16)[
        inverse
    ]
    own_heads = jnp.stack(
        [
            jnp.sum(gradients[2], axis=0),
            jnp.sum(gradients[3], axis=0),
            jnp.sum(gradients[4], axis=0),
        ]
    )
    head_grads = lax.all_gather(own_heads, "dp", axis=1, tiled=True)
    gain_grad = jnp.sum(gradients[5], axis=0)
    return (grad_inputs, state_grad, gain_grad, head_grads)


def solution(mesh):
    in_specs = (
        P(("groups", "dp"), None),
        P(("groups", "dp"), None),
        P(("groups", "dp"), None),
        P(("groups", "dp"), None),
        P(("groups", "dp"), None),
        P(("groups", "dp"), None),
        P(),
        P(),
        P(),
        P(),
        P("groups", "dp", None, None),
        P(("groups", "dp")),
        P("groups"),
    )
    out_specs = (
        P(("groups", "dp"), None),
        P("groups", "dp", None, None),
        P(("groups", "dp")),
        P("groups", None),
    )
    return jax.shard_map(local, mesh=mesh, in_specs=in_specs, out_specs=out_specs, check_vma=False)
```

profile of v0, /device:TPU:9, one launch (start us, length us, event | category | flops | bytes accessed | tf_op | source)
XLA Modules:
  0.0 391.7 jit_solution(12096214340189381911)
XLA Ops:
  8.6 6.6 %all-to-all-start = ((bf16[256,16,4]{0,2,1:T(4,128)(2,1)}), bf16[256,16,4]{0,2,1:T(4,128)(2,1)S(1)}, u32[]{:S(2)}, u32[]{:S(2)}) async-start(bf16[256,16,4]{0,2,1:T(4,128)(2,1)} %all_to_all.54), calls=%async_computation | async-start | bytes 65536 | tf_op jit(solution)/shard_map/all_to_all | solution.py:185
  15.1 4.1 %copy.107 = bf16[256,4096]{0,1:T(8,128)(2,1)} copy(bf16[256,4096]{1,0:T(8,128)(2,1)} %param.14) | data formatting | bytes 4194304 | tf_op jit(solution)/shard_map/all_to_all | solution.py:183
  20.2 5.2 %all-to-all-start.3 = ((bf16[256,16,256]{0,2,1:T(8,128)(2,1)}), bf16[256,16,256]{0,2,1:T(8,128)(2,1)S(1)}, u32[]{:S(2)}, u32[]{:S(2)}) async-start(bf16[256,16,256]{0,2,1:T(8,128)(2,1)} %bitcast.249), calls=%async_computation.3 | async-start | bytes 4194304 | tf_op jit(solution)/shard_map/all_to_all | solution.py:183
  26.2 4.1 %copy.106 = bf16[256,4096]{0,1:T(8,128)(2,1)} copy(bf16[256,4096]{1,0:T(8,128)(2,1)} %param.13) | data formatting | bytes 4194304 | tf_op jit(solution)/shard_map/all_to_all | solution.py:182
  30.3 46.6 %all-to-all-done.3 = bf16[256,16,256]{0,2,1:T(8,128)(2,1)S(1)} async-done(((bf16[256,16,256]{0,2,1:T(8,128)(2,1)}), bf16[256,16,256]{0,2,1:T(8,128)(2,1)S(1)}, u32[]{:S(2)}, u32[]{:S(2)}) %all-to-all-start.3) | async-done | bytes 2097184 | tf_op jit(solution)/shard_map/all_to_all | solution.py:183
  76.9 6.9 %all-to-all-start.2 = ((bf16[256,16,256]{0,2,1:T(8,128)(2,1)}), bf16[256,16,256]{0,2,1:T(8,128)(2,1)}, u32[]{:S(2)}, u32[]{:S(2)}) async-start(bf16[256,16,256]{0,2,1:T(8,128)(2,1)} %bitcast.247), calls=%async_computation.2 | async-start | bytes 4194304 | tf_op jit(solution)/shard_map/all_to_all | solution.py:182
  84.6 63.3 %all-gather = s32[16,1,256]{2,1,0:T(1,128)S(1)} all-gather(s32[1,1,256]{2,1,0:T(1,128)S(1)} %bitcast.271), channel_id=1, replica_groups=mesh['groups'=2,'dp'=16] {'dp'}, dimensions={0}, use_global_device_ids=true | all-gather | bytes 17408 | tf_op jit(solution)/shard_map/all_gather | solution.py:191
  149.4 4.1 %copy.105 = bf16[256,4096]{0,1:T(8,128)(2,1)} copy(bf16[256,4096]{1,0:T(8,128)(2,1)} %param.18) | data formatting | bytes 4194304 | tf_op jit(solution)/shard_map/all_to_all | solution.py:184
  153.4 5.3 %gather_fusion = bf16[64,4,64,128]{3,2,1,0:T(8,128)(2,1)} fusion(bf16[64,4,64,128]{3,2,1,0:T(8,128)(2,1)} %param.23, s32[1024]{0:T(1024)S(1)} %pad_clamp_fusion.1), kind=kCustom, calls=%fused_computation | custom fusion | bytes 8388864 | tf_op jit(solution)/shard_map/gather | solution.py:197
  163.3 4.9 %fusion.64 = f32[16,4,64,256]{3,2,1,0:T(8,128)} fusion(bf16[16,256,128,1]{2,1,3,0:T(8,128)(2,1)} %bitcast.253), kind=kOutput, calls=%fused_computation.90 | convolution fusion | flops 1610612736 | bytes 5242880 | tf_op jit(solution)/shard_map/vmap(jvp())/while/body/eval_jaxpr/hpn,tn->thp/dot_general | solution.py:85
  168.2 4.3 %fusion.99 = f32[16,256,256]{2,1,0:T(8,128)} fusion(bf16[16,256,128]{2,1,0:T(8,128)(2,1)} %bitcast.254, bf16[16,256,128]{2,1,0:T(8,128)(2,1)} %bitcast.257), kind=kOutput, calls=%fused_computation.162 | convolution fusion | flops 268435456 | bytes 6291456 | tf_op jit(solution)/shard_map/vmap(jvp())/while/body/eval_jaxpr/dot_general | solution.py:79
  172.6 5.7 %bitcast_convert_fusion = bf16[16,256,4,64]{1,3,2,0:T(8,128)(2,1)} fusion(bf16[16,4,4,64,128]{4,3,2,1,0:T(8,128)(2,1)S(1)} %bitcast.252, pred[16,256,4]{1,2,0:T(4,128)(4,1)S(1)} %iota_compare_fusion.1, bf16[16,256,128]{2,1,0:T(8,128)(2,1)S(1)} %bitcast.255), kind=kOutput, calls=%fused_computation.52 | convolution fusion | flops 1076887552 | bytes 7356416 | tf_op jit(solution)/shard_map/vmap(tgn,ghpn->thp)/dot_general | solution.py:16
  184.7 6.2 %fusion.48 = (f32[16,256,4]{1,2,0:T(4,128)S(1)}, f32[16,4,64,256]{3,2,1,0:T(8,128)}) fusion(bf16[256,16,256]{0,2,1:T(8,128)(2,1)} %all-to-all-done.2, bf16[16,256,128,1]{2,1,3,0:T(8,128)(2,1)} %bitcast.258), kind=kOutput, calls=%fused_computation.73 | convolution fusion | flops 1613742080 | bytes 7405568 | tf_op jit(solution)/shard_map/vmap(transpose(jvp()))/while/body/eval_jaxpr/sh,shp,sn->hpn/dot_general | solution.py:95
  196.3 16.8 %multiply_reduce_fusion.2 = (f32[16,256,4]{1,2,0:T(4,128)S(1)}, f32[16,256,4,64]{1,3,2,0:T(8,128)}, f32[16,256,4,64]{1,3,2,0:T(8,128)}) fusion(f32[16,256,4,64]{1,3,2,0:T(8,128)S(1)} %bitcast.250, f32[16,256,4,64]{1,3,2,0:T(8,128)S(1)} %bitcast.251, f32[4]{0:T(128)S(1)} %copy-done.36, bf16[16,256,4,64]{1,3,2,0:T(8,128)(2,1)S(1)} %copy-done.12, ...), kind=kOutput, calls=%fused_computation.78 | convolution fusion | flops 3252666368 | bytes 30736400 | tf_op jit(solution)/shard_map/vmap(jvp())/while/body/eval_jaxpr/tsh,shp->thp/dot_general | solution.py:81
  213.2 5.9 %fusion.2 = f32[16,256,4]{1,2,0:T(4,128)} fusion(f32[16,256,4]{1,2,0:T(4,128)S(1)} %select_reduce_fusion, f32[16,256,4]{1,2,0:T(4,128)S(1)} %get-tuple-element.439, pred[16,256,256]{2,1,0:T(8,128)(4,1)S(1)} %compare_and_fusion), kind=kLoop, calls=%fused_computation.6 | loop fusion | flops 16760832 | bytes 1245184 | tf_op jit(solution)/shard_map/vmap(jvp())/while/body/eval_jaxpr/reduce_sum | solution.py:78
  219.1 11.7 %all-to-all-done.1 = bf16[256,16,256]{0,2,1:T(8,128)(2,1)S(1)} async-done(((bf16[256,16,256]{0,2,1:T(8,128)(2,1)}), bf16[256,16,256]{0,2,1:T(8,128)(2,1)S(1)}, u32[]{:S(2)}, u32[]{:S(2)}) %all-to-all-start.1) | async-done | bytes 2097184 | tf_op jit(solution)/shard_map/all_to_all | solution.py:184
  240.4 28.3 %fusion.28 = (f32[16,256,4]{1,2,0:T(4,128)S(1)}, f32[16,256,4]{1,2,0:T(4,128)S(1)}, f32[16,256,4]{1,2,0:T(4,128)}, f32[16,256,4]{1,2,0:T(4,128)S(1)}, f32[16,256,256,4]{2,1,3,0:T(8,128)}) fusion(f32[16,256,4]{1,2,0:T(4,128)S(1)} %bitcast.261, f32[16,256,256]{2,1,0:T(8,128)S(1)} %copy-done.7, f32[16,256,4]{1,2,0:T(4,128)S(1)} %copy-done.23, ...), kind=kOutput, calls=%fused_computation.42 | convolution fusion | flops 3292463104 | bytes 28966912 | tf_op jit(solution)/shard_map/vmap(transpose(jvp()))/while/body/eval_jaxpr/tsh,shp->thp/dot_general | solution.py:81
  269.5 9.9 %reduce-window.28 = f32[16,4,2,128]{3,0,1,2:T(8,128)S(1)} reduce-window(f32[16,4,2,128]{3,0,1,2:T(8,128)S(1)} %copy.91, f32[]{:T(128)} %constant.180.clone.1), window={size=1x1x1x128 pad=0_0x0_0x0_0x0_127}, to_apply=%region_14.15 | reduce-window | flops 2080768 | bytes 131076 | tf_op jit(solution)/shard_map/reduce-window
  282.8 19.1 %fusion.38 = bf16[16,256,4,64]{1,3,2,0:T(8,128)(2,1)} fusion(f32[16,4,64,256]{3,2,1,0:T(8,128)} %get-tuple-element.442, f32[16,256,4,64]{1,3,2,0:T(8,128)} %copy-done.5, f32[4]{0:T(128)} %dynamic_slice.104, f32[16,256,4]{1,2,0:T(4,128)S(1)} %get-tuple-element.437, f32[16,256,4]{1,2,0:T(4,128)} %copy-done.22, f32[16,256,256]{2,1,0:T(8,128)} %fusion.99, ...), kind=kOutput, calls=%fused_computation.57 | convolution fusion | flops 3243245568 | bytes 15925264 | tf_op jit(solution)/shard_map/vmap(transpose(jvp()))/while/body/eval_jaxpr/tsh,shp->thp/dot_general | solution.py:81
  301.9 6.3 %all-to-all-start.4 = ((bf16[16,256,256]{1,2,0:T(8,128)(2,1)}), bf16[16,256,256]{1,2,0:T(8,128)(2,1)}, u32[]{:S(2)}, u32[]{:S(2)}) async-start(bf16[16,256,256]{1,2,0:T(8,128)(2,1)} %bitcast.259), calls=%async_computation.4 | async-start | bytes 4194304 | tf_op jit(solution)/shard_map/all_to_all | solution.py:221
  310.3 5.0 %fusion.37 = f32[256]{0:T(256)S(1)} fusion(f32[16,256,4,64]{1,3,2,0:T(8,128)} %get-tuple-element.443, f32[256]{0:T(256)S(1)} %dynamic_slice.105, f32[16,256,4]{1,2,0:T(4,128)S(1)} %multiply_multiply_fusion, f32[16,256,4]{1,2,0:T(4,128)S(1)} %fusion.87, bf16[256,16,256]{0,2,1:T(8,128)(2,1)} %all-to-all-done.2, bf16[256,16,256]{0,2,1:T(8,128)(2,1)} %copy-done, ...), kind=kLoop, calls=%fused_computation.51 | loop fusion | flops 16776960 | bytes 10618880 | tf_op jit(solution)/shard_map/reduce_sum | solution.py:233
  315.8 50.2 %all-gather.1 = f32[16,4,3]{2,1,0:T(4,128)S(1)} all-gather(f32[1,4,3]{2,1,0:T(4,128)S(1)} %bitcast.266), channel_id=1, replica_groups=mesh['groups'=2,'dp'=16] {'dp'}, dimensions={0}, use_global_device_ids=true | all-gather | bytes 816 | tf_op jit(solution)/shard_map/all_gather | solution.py:236
  366.7 5.3 %convert_bitcast_fusion = bf16[16,4,4,64,128]{4,3,1,2,0:T(8,128)(2,1)S(1)} fusion(pred[16,256,4]{1,2,0:T(4,128)(4,1)S(1)} %copy-done.25, f32[16,256,4,64]{1,3,2,0:T(8,128)} %copy-done.5, bf16[16,256,128]{2,1,0:T(8,128)(2,1)S(1)} %bitcast.256, f32[16,256,4]{1,2,0:T(4,128)S(1)} %copy-done.19), kind=kOutput, calls=%fused_computation.75 | convolution fusion | flops 1080033280 | bytes 9519104 | tf_op jit(solution)/shard_map/vmap(tgn,thp->ghpn)/dot_general | solution.py:24
  375.5 5.3 %gather_fusion.1 = bf16[64,4,64,128]{3,2,1,0:T(8,128)(2,1)} fusion(bf16[64,4,64,128]{3,2,1,0:T(8,128)(2,1)} %bitcast.246, s32[1024]{0:T(1024)S(1)} %pad_clamp_fusion), kind=kCustom, calls=%fused_computation.1 | custom fusion | bytes 8388864 | tf_op jit(solution)/shard_map/gather | solution.py:226
  (143 shorter events, 46.1 us)
Async XLA Ops:
  8.6 11.6 %all-to-all-start = ((bf16[256,16,4]{0,2,1:T(4,128)(2,1)}), bf16[256,16,4]{0,2,1:T(4,128)(2,1)S(1)}, u32[]{:S(2)}, u32[]{:S(2)}) async-start(bf16[256,16,4]{0,2,1:T(4,128)(2,1)} %all_to_all.54), calls=%async_computation | async-start | bytes 65536 | tf_op jit(solution)/shard_map/all_to_all | solution.py:185
  20.2 170.8 %copy-start.14 = (bf16[256,16,4]{0,2,1:T(4,128)(2,1)}, bf16[256,16,4]{0,2,1:T(4,128)(2,1)S(1)}, u32[]{:S(2)}) copy-start(bf16[256,16,4]{0,2,1:T(4,128)(2,1)S(1)} %all-to-all-done) | copy-start | bytes 98308
  20.2 56.7 %all-to-all-start.3 = ((bf16[256,16,256]{0,2,1:T(8,128)(2,1)}), bf16[256,16,256]{0,2,1:T(8,128)(2,1)S(1)}, u32[]{:S(2)}, u32[]{:S(2)}) async-start(bf16[256,16,256]{0,2,1:T(8,128)(2,1)} %bitcast.249), calls=%async_computation.3 | async-start | bytes 4194304 | tf_op jit(solution)/shard_map/all_to_all | solution.py:183
  25.4 137.9 %all-gather.7.cloned.1.call-start = ((), (), s32[]{:S(2)}) async-start(), calls=%async_computation.6 | async-start | bytes 1114112 | tf_op jit(solution)/shard_map/all_gather | solution.py:189
  26.1 58.4 %copy-start.34 = (s32[64]{0:T(128)S(1)}, s32[64]{0:T(128)}, u32[]{:S(2)}) copy-start(s32[64]{0:T(128)} %param.25) | copy-start | bytes 772
  26.1 58.4 %copy-start.30 = (s32[256]{0:T(256)S(1)}, s32[256]{0:T(256)}, u32[]{:S(2)}) copy-start(s32[256]{0:T(256)} %param.24) | copy-start | bytes 3076
  26.2 121.7 %copy-start.32 = (f32[64]{0:T(128)S(1)}, f32[64]{0:T(128)}, u32[]{:S(2)}) copy-start(f32[64]{0:T(128)} %param.19) | copy-start | bytes 772
  26.2 121.8 %copy-start.33 = (f32[64]{0:T(128)S(1)}, f32[64]{0:T(128)}, u32[]{:S(2)}) copy-start(f32[64]{0:T(128)} %param.21) | copy-start | bytes 772
  76.9 101.4 %copy-start = (bf16[256,16,256]{0,2,1:T(8,128)(2,1)}, bf16[256,16,256]{0,2,1:T(8,128)(2,1)S(1)}, u32[]{:S(2)}) copy-start(bf16[256,16,256]{0,2,1:T(8,128)(2,1)S(1)} %all-to-all-done.3) | copy-start | bytes 6291460
  76.9 103.8 %all-to-all-start.2 = ((bf16[256,16,256]{0,2,1:T(8,128)(2,1)}), bf16[256,16,256]{0,2,1:T(8,128)(2,1)}, u32[]{:S(2)}, u32[]{:S(2)}) async-start(bf16[256,16,256]{0,2,1:T(8,128)(2,1)} %bitcast.247), calls=%async_computation.2 | async-start | bytes 4194304 | tf_op jit(solution)/shard_map/all_to_all | solution.py:182
  83.8 84.4 %all-gather.5.cloned.1.call-start = ((), (), s32[]{:S(2)}) async-start(), calls=%async_computation.5 | async-start | bytes 1114112 | tf_op jit(solution)/shard_map/all_gather | solution.py:188
  147.9 43.0 %copy-start.27 = (f32[4]{0:T(128)}, f32[4]{0:T(128)S(1)}, u32[]{:S(2)}) copy-start(f32[4]{0:T(128)S(1)} %dynamic_slice.103) | copy-start | bytes 52
  159.4 13.2 %copy-start.24 = (pred[16,256,4]{1,2,0:T(4,128)(4,1)}, pred[16,256,4]{1,2,0:T(4,128)(4,1)S(1)}, u32[]{:S(2)}) copy-start(pred[16,256,4]{1,2,0:T(4,128)(4,1)S(1)} %iota_compare_fusion.1) | copy-start | bytes 49156
  180.7 50.1 %all-to-all-start.1 = ((bf16[256,16,256]{0,2,1:T(8,128)(2,1)}), bf16[256,16,256]{0,2,1:T(8,128)(2,1)S(1)}, u32[]{:S(2)}, u32[]{:S(2)}) async-start(bf16[256,16,256]{0,2,1:T(8,128)(2,1)} %bitcast.248), calls=%async_computation.1 | async-start | bytes 4194304 | tf_op jit(solution)/shard_map/all_to_all | solution.py:184
  184.7 11.6 %copy-start.6 = (f32[16,256,256]{2,1,0:T(8,128)S(1)}, f32[16,256,256]{2,1,0:T(8,128)}, u32[]{:S(2)}) copy-start(f32[16,256,256]{2,1,0:T(8,128)} %fusion.99) | copy-start | bytes 12582916
  184.7 11.6 %copy-start.8 = (f32[256,16,256]{0,2,1:T(8,128)S(1)}, f32[256,16,256]{0,2,1:T(8,128)}, u32[]{:S(2)}) copy-start(f32[256,16,256]{0,2,1:T(8,128)} %convert_element_type.148) | copy-start | bytes 12582916
  191.8 21.4 %copy-start.22 = (f32[16,256,4]{1,2,0:T(4,128)}, f32[16,256,4]{1,2,0:T(4,128)S(1)}, u32[]{:S(2)}) copy-start(f32[16,256,4]{1,2,0:T(4,128)S(1)} %get-tuple-element.440) | copy-start | bytes 196612
  194.2 19.0 %copy-start.17 = (f32[16,256,4]{1,2,0:T(4,128)}, f32[16,256,4]{1,2,0:T(4,128)S(1)}, u32[]{:S(2)}) copy-start(f32[16,256,4]{1,2,0:T(4,128)S(1)} %get-tuple-element.433) | copy-start | bytes 196612
  213.2 22.2 %copy-start.16 = (f32[16,256,4]{1,2,0:T(4,128)}, f32[16,256,4]{1,2,0:T(4,128)S(1)}, u32[]{:S(2)}) copy-start(f32[16,256,4]{1,2,0:T(4,128)S(1)} %get-tuple-element.430) | copy-start | bytes 196612
  240.3 28.4 %copy-start.5 = (f32[16,256,4,64]{1,3,2,0:T(8,128)}, f32[16,256,4,64]{1,3,2,0:T(8,128)S(1)}, u32[]{:S(2)}) copy-start(f32[16,256,4,64]{1,3,2,0:T(8,128)S(1)} %get-tuple-element.429) | copy-start | bytes 12582916
  301.9 78.8 %all-to-all-start.4 = ((bf16[16,256,256]{1,2,0:T(8,128)(2,1)}), bf16[16,256,256]{1,2,0:T(8,128)(2,1)}, u32[]{:S(2)}, u32[]{:S(2)}) async-start(bf16[16,256,256]{1,2,0:T(8,128)(2,1)} %bitcast.259), calls=%async_computation.4 | async-start | bytes 4194304 | tf_op jit(solution)/shard_map/all_to_all | solution.py:221
  310.3 56.4 %copy-start.11 = (bf16[4096,128]{1,0:T(8,128)(2,1)S(1)}, bf16[4096,128]{1,0:T(8,128)(2,1)}, u32[]{:S(2)}) copy-start(bf16[4096,128]{1,0:T(8,128)(2,1)} %all-gather.7.cloned.1.call-done) | copy-start | bytes 3145732
  310.3 56.4 %copy-start.19 = (f32[16,256,4]{1,2,0:T(4,128)S(1)}, f32[16,256,4]{1,2,0:T(4,128)}, u32[]{:S(2)}) copy-start(f32[16,256,4]{1,2,0:T(4,128)} %copy-done.17) | copy-start | bytes 196612
  310.3 56.4 %copy-start.25 = (pred[16,256,4]{1,2,0:T(4,128)(4,1)S(1)}, pred[16,256,4]{1,2,0:T(4,128)(4,1)}, u32[]{:S(2)}) copy-start(pred[16,256,4]{1,2,0:T(4,128)(4,1)} %copy-done.24) | copy-start | bytes 49156
  (20 other events, 82.3 us)
Sparse Core Ops, SparseCore 0:
  28.4 51.8 all-gather.6
  86.8 51.8 all-gather.4
where the time goes:
time: 393 us; the launch traced here: 392 us
  blocking collectives  113 us (29%)
  matrix products  90.7 us (23%)
  waiting for transfers between devices  60.7 us (15%)
  other arithmetic  44.7 us (11%)
  local copies, waits for them, and re-layouts  38.5 us (10%)
  starting transfers between devices  29 us (7%)
  between operations  14.7 us (4%)
    dot_general x3, matrix products, advance(): local_part = jnp.einsum('tsh,shp->thp', weights, block_x, precision=highest)  64.2 us
    all_gather x1, blocking collectives, local(): turns_all = lax.all_gather(turn_index, 'dp', axis=0, tiled=True)  63.3 us
    all_gather x1, blocking collectives, local(): head_grads = lax.all_gather(own_heads, 'dp', axis=1, tiled=True)  50.2 us
    all_to_all x1, waiting for transfers between devices, local(): lax.all_to_all(gate_values, 'dp', split_axis=1, concat_axis=0, tiled=True)  46.6 us
    another operation x5, other arithmetic  12.3 us
    all_to_all x1, waiting for transfers between devices, local(): lax.all_to_all(cotangent, 'dp', split_axis=1, concat_axis=0, tiled=True)  11.7 us
  transfers between devices with their start and end apart: 7, of which 3 were waited for; matrix products, arithmetic and copies ran while one was open for 25% of the time, Pallas kernels for 0%

commit v1 on v0

v1 whole, which is shorter than its diff:
```python
import functools

import jax
import jax.numpy as jnp
from jax import lax
from jax.experimental import pallas as pl
from jax.experimental.pallas import tpu as pltpu
from jax.sharding import PartitionSpec as P


TMAX = 4
EPS = 1e-5
LOG2E = 1.4426950408889634
F32 = jnp.float32
BF16 = jnp.bfloat16
HIGHEST = lax.Precision.HIGHEST
TURN_ROWS = 16


def nt_dot(a, b):
    return lax.dot_general(a, b, (((1,), (1,)), ((), ())), preferred_element_type=F32)


def nn_dot(a, b):
    return jnp.dot(a, b, preferred_element_type=F32)


def any_spec():
    return pl.BlockSpec(memory_space=pl.ANY)


def vmem_spec():
    return pl.BlockSpec(memory_space=pltpu.VMEM)


def smem_spec():
    return pl.BlockSpec(memory_space=pltpu.SMEM)


def bank_kernel(count, me_ref, slot_ref, bank_ref, out_ref, sem):
    me = me_ref[0]

    def copy(i):
        device = lax.bitwise_xor(me, 2 * (i // TMAX) + 1)
        slot = slot_ref[device * TMAX + i % TMAX]
        return pltpu.make_async_copy(bank_ref.at[slot], out_ref.at[i], sem.at[i])

    for i in range(count):
        copy(i).start()
    for i in range(count):
        copy(i).wait()


def pick_states(me, slots, bank):
    chips = slots.shape[0] // TMAX // 2
    count = chips * TMAX
    return pl.pallas_call(
        functools.partial(bank_kernel, count),
        out_shape=jax.ShapeDtypeStruct((count,) + bank.shape[1:], BF16),
        in_specs=[smem_spec(), smem_spec(), any_spec()],
        out_specs=vmem_spec(),
        scratch_shapes=[pltpu.SemaphoreType.DMA((count,))],
        cost_estimate=pl.CostEstimate(flops=0, transcendentals=0, bytes_accessed=4 * count * bank.shape[1] * bank.shape[2]),
        name="pick_states",
    )(me, slots, bank)


def turn_row(packed_ref, rows):
    pieces = [packed_ref[rows + i : rows + i + 1, :].astype(F32) for i in range(rows // 128)]
    return jnp.concatenate(pieces, axis=1)


def start_kernel(chips, width, rows, order, me_ref, slot_ref, bank_ref, lent_ref, *refs):
    packed = refs[:chips]
    outs = refs[chips : 2 * chips]
    all_ref, own, lent, sem, lent_sem, pack_sem = refs[2 * chips :]
    me = me_ref[0]
    core = lax.rem(me, 2)

    def pack_copy(j):
        return pltpu.make_async_copy(packed[j], all_ref.at[j], pack_sem.at[j])

    def copy(i):
        device = lax.bitwise_xor(me, 2 * (i // TMAX))
        slot = slot_ref[device * TMAX + i % TMAX]
        return pltpu.make_async_copy(bank_ref.at[slot], own.at[i], sem.at[i])

    def lent_copy(j):
        part = pl.ds(j * TMAX, TMAX)
        return pltpu.make_async_copy(lent_ref.at[part], lent.at[part], lent_sem.at[j])

    for j in order:
        pack_copy(j).start()
        for i in range(j * TMAX, (j + 1) * TMAX):
            copy(i).start()
        lent_copy(j).start()
    mine = pl.ds(pl.multiple_of(core * width, width), width)
    other = pl.ds(pl.multiple_of((1 - core) * width, width), width)
    for j in order:
        pack_copy(j).wait()
        proj = all_ref[j, :rows, :]
        turn = turn_row(all_ref.at[j], rows)
        for i in range(j * TMAX, (j + 1) * TMAX):
            copy(i).wait()
        lent_copy(j).wait()
        for source, place in ((own, mine), (lent, other)):
            total = jnp.zeros((width, rows), F32)
            for g in range(TMAX):
                part = nt_dot(source[j * TMAX + g], proj)
                total = jnp.where(turn == float(g), part, total)
            outs[j][place, :] = total.astype(BF16)


def start_reads(me, slots, bank, lent, packed, rows, order):
    chips = len(packed)
    width, state = bank.shape[1:]
    out_shape = [jax.ShapeDtypeStruct((2 * width, rows), BF16)] * chips
    out_shape.append(jax.ShapeDtypeStruct((chips,) + packed[0].shape, BF16))
    results = pl.pallas_call(
        functools.partial(start_kernel, chips, width, rows, order),
        out_shape=out_shape,
        in_specs=[smem_spec(), smem_spec()] + [any_spec()] * (chips + 2),
        out_specs=[vmem_spec()] * (chips + 1),
        scratch_shapes=[
            pltpu.VMEM((chips * TMAX, width, state), BF16),
            pltpu.VMEM((chips * TMAX, width, state), BF16),
            pltpu.SemaphoreType.DMA((chips * TMAX,)),
            pltpu.SemaphoreType.DMA((chips,)),
            pltpu.SemaphoreType.DMA((chips,)),
        ],
        cost_estimate=pl.CostEstimate(
            flops=2 * chips * TMAX * 2 * width * state * rows,
            transcendentals=0,
            bytes_accessed=chips * (TMAX * width * state * 4 + width * rows * 4),
        ),
        name="start_reads",
    )(me, slots, bank, lent, *packed)
    return results[:chips], results[chips]


def mix_kernel(
    chip_xor,
    heads,
    hdim,
    rows,
    me_ref,
    skip_ref,
    x_ref,
    gate_ref,
    cot_ref,
    inner_ref,
    source_ref,
    gain_ref,
    score_ref,
    begin_ref,
    *refs,
):
    same_ref, other_ref, grad_ref, stats_ref, gain_out_ref, high_ref, low_ref, begins, sem = refs[-9:]
    half = pl.program_id(0)
    width = heads * hdim
    device = lax.bitwise_xor(me_ref[0], 2 * chip_xor + half)
    fetch = pltpu.make_async_copy(begin_ref, begins, sem)

    @pl.when(half == 0)
    def _():
        fetch.start()

    mid = rows // 2
    x_t = x_ref[...].T
    gate_t = gate_ref[...].T
    cot_t = cot_ref[...].T
    gain_rows = jnp.broadcast_to(gain_ref[...], (8, width)).T
    inner = inner_ref[0]
    pad = jnp.zeros((8 - heads, rows), F32)
    source_cols = jnp.concatenate([source_ref[0], pad], axis=0).T

    @pl.when(half == 0)
    def _():
        fetch.wait()

    begin_rows = begins[pl.ds(pl.multiple_of(lax.rem(device, 2) * width, width), width), :]
    reads = []
    grads = []
    gains = []
    for h in range(heads):
        span = slice(h * hdim, (h + 1) * hdim)
        skip = skip_ref[device * heads + h]
        x_b = x_t[span]
        x = x_b.astype(F32)
        row = inner[h : h + 1, :]
        col = source_cols[:, h : h + 1]
        for low, high in ((0, 0), (0, 1), (1, 1)):
            source = slice(low * mid, (low + 1) * mid)
            target = slice(high * mid, (high + 1) * mid)
            weight = jnp.exp2(jnp.minimum(row[:, target] - col[source], 64.0)) * score_ref[source, target]
            rounded = weight.astype(BF16)
            high_ref[h, source, target] = rounded
            low_ref[source, target] = (weight - rounded.astype(F32)).astype(BF16)
        high_ref[h, mid:, :mid] = jnp.zeros((mid, mid), BF16)
        low_ref[mid:, :mid] = jnp.zeros((mid, mid), BF16)
        local = nn_dot(x_b, high_ref[h])
        grown = jnp.exp2(row)
        begin = grown * begin_rows[span].astype(F32)
        y = local + nn_dot(x_b, low_ref[...]) + begin + skip * x
        gate = gate_t[span].astype(F32)
        silu = gate / (1.0 + jnp.exp(-gate))
        gated = y * silu
        square = jnp.sum(gated * gated, axis=0, keepdims=True) * (1.0 / hdim)
        scale = lax.rsqrt(square + EPS)
        normed = gated * scale
        cot = cot_t[span].astype(F32)
        gains.append(cot * normed)
        dn = cot * gain_rows[span, 0:1]
        along = jnp.sum(dn * normed, axis=0, keepdims=True) * (1.0 / hdim)
        dy = (dn - normed * along) * scale * silu
        reads.append((grown * dy).astype(BF16))
        dy_b = dy.astype(BF16)
        d_x = nt_dot(dy_b, high_ref[h])
        grads.append((skip * dy + d_x).astype(BF16))
        taken = jnp.sum(x * d_x, axis=0, keepdims=True)
        given = jnp.sum(begin * dy + dy_b.astype(F32) * local, axis=0, keepdims=True)
        stats_ref[0, h, 0:1, :] = given - taken
        stats_ref[0, h, 1:2, :] = taken
        stats_ref[0, h, 2:3, :] = jnp.sum(x * dy, axis=0, keepdims=True)
        stats_ref[0, h, 3:8, :] = jnp.zeros((5, rows), F32)
    read = jnp.concatenate(reads, axis=0)

    @pl.when(half == 0)
    def _():
        same_ref[...] = read

    @pl.when(half == 1)
    def _():
        other_ref[...] = read

    grad_ref[...] = jnp.concatenate(grads, axis=0).T
    gain_part = jnp.concatenate(gains, axis=0)
    ones = jnp.ones((8, rows), BF16)
    gain_high = gain_part.astype(BF16)
    gain_low = (gain_part - gain_high.astype(F32)).astype(BF16)
    gain_out_ref[...] = nt_dot(ones, gain_high) + nt_dot(ones, gain_low)


def mix(me, chip_xor, skip, x, gate, cot, begin, inner, source, gain, score, previous, heads, hdim):
    rows, channels = x.shape
    width = heads * hdim
    devices = channels // width

    def device(half, me_ref):
        return lax.bitwise_xor(me_ref[0], 2 * chip_xor + half)

    columns = pl.BlockSpec((rows, width), lambda i, p: (0, device(i, p)))
    per_head = pl.BlockSpec((1, heads, rows), lambda i, p: (device(i, p), 0, 0))
    gain_spec = pl.BlockSpec((1, width), lambda i, p: (0, device(i, p)))
    whole = pl.BlockSpec((width, rows), lambda i, p: (0, 0))
    in_specs = [
        pl.BlockSpec(memory_space=pltpu.SMEM),
        columns,
        columns,
        columns,
        per_head,
        per_head,
        gain_spec,
        pl.BlockSpec((rows, rows), lambda i, p: (0, 0)),
        any_spec(),
    ]
    operands = [skip, x, gate, cot, inner, source, gain, score, begin]
    aliases = {}
    if previous is not None:
        for i, value in enumerate(previous):
            aliases[1 + len(operands)] = 2 + i
            operands.append(value)
            in_specs.append(any_spec())
    results = pl.pallas_call(
        functools.partial(mix_kernel, chip_xor, heads, hdim, rows),
        out_shape=[
            jax.ShapeDtypeStruct((width, rows), BF16),
            jax.ShapeDtypeStruct((width, rows), BF16),
            jax.ShapeDtypeStruct((rows, channels), BF16),
            jax.ShapeDtypeStruct((devices, heads, 8, rows), F32),
            jax.ShapeDtypeStruct((8, channels), F32),
        ],
        grid_spec=pltpu.PrefetchScalarGridSpec(
            num_scalar_prefetch=1,
            grid=(2,),
            in_specs=in_specs,
            out_specs=[
                whole,
                whole,
                columns,
                pl.BlockSpec((1, heads, 8, rows), lambda i, p: (device(i, p), 0, 0, 0)),
                pl.BlockSpec((8, width), lambda i, p: (0, device(i, p))),
            ],
            scratch_shapes=[
                pltpu.VMEM((heads, rows, rows), BF16),
                pltpu.VMEM((rows, rows), BF16),
                pltpu.VMEM((2 * width, rows), BF16),
                pltpu.SemaphoreType.DMA,
            ],
        ),
        input_output_aliases=aliases,
        cost_estimate=pl.CostEstimate(
            flops=12 * rows * rows * width,
            transcendentals=2 * heads * rows * rows,
            bytes_accessed=24 * rows * width,
        ),
        name="mix",
    )(me, *operands)
    return results[0], results[1], tuple(results[2:])


def state_kernel(partners, rows, me_ref, slot_ref, same_ref, other_ref, *refs):
    count = len(partners)
    reads = refs[:count]
    out_ref, buffer, held, packs, sem, read_sem, pack_sem = refs[-7:]
    me = me_ref[0]

    def copy(i, g):
        slot = slot_ref[lax.bitwise_xor(me, partners[i]) * TMAX + g]
        return pltpu.make_async_copy(buffer.at[i * TMAX + g], out_ref.at[slot], sem.at[i * TMAX + g])

    def read_copy(i):
        return pltpu.make_async_copy(reads[i], held.at[i], read_sem.at[i])

    def pack_copy(i):
        source = (other_ref if partners[i] % 2 else same_ref).at[partners[i] // 2]
        return pltpu.make_async_copy(source, packs.at[i], pack_sem.at[i])

    for i in range(count):
        read_copy(i).start()
        pack_copy(i).start()
    for i in range(count):
        read_copy(i).wait()
        pack_copy(i).wait()
        read = held[i].astype(F32)
        turn = turn_row(packs.at[i], rows)
        proj = packs[i, :rows, :]
        for g in range(TMAX):
            masked = jnp.where(turn == float(g), read, 0.0).astype(BF16)
            buffer[i * TMAX + g] = nn_dot(masked, proj).astype(BF16)
            copy(i, g).start()
    for i in range(count):
        for g in range(TMAX):
            copy(i, g).wait()


def state_grads(me, slots, partners, reads, packed_same, packed_other, previous, shape):
    width, rows = reads[0].shape
    count = len(partners)
    operands = [me, slots, packed_same, packed_other, *reads]
    in_specs = [smem_spec(), smem_spec()] + [any_spec()] * (count + 2)
    aliases = {}
    if previous is not None:
        aliases[len(operands)] = 0
        operands.append(previous)
        in_specs.append(any_spec())
    return pl.pallas_call(
        functools.partial(state_kernel, partners, rows),
        out_shape=jax.ShapeDtypeStruct(shape, BF16),
        in_specs=in_specs,
        out_specs=any_spec(),
        scratch_shapes=[
            pltpu.VMEM((count * TMAX,) + shape[1:], BF16),
            pltpu.VMEM((count, width, rows), BF16),
            pltpu.VMEM((count,) + packed_same.shape[1:], BF16),
            pltpu.SemaphoreType.DMA((count * TMAX,)),
            pltpu.SemaphoreType.DMA((count,)),
            pltpu.SemaphoreType.DMA((count,)),
        ],
        input_output_aliases=aliases,
        cost_estimate=pl.CostEstimate(
            flops=2 * count * TMAX * shape[1] * shape[2] * rows,
            transcendentals=0,
            bytes_accessed=count * (2 * TMAX * shape[1] * shape[2] + 4 * shape[1] * rows),
        ),
        name="state_grads",
    )(*operands)


def chip_order(chips):
    far = sorted(range(chips // 2, chips), key=lambda j: (j.bit_count(), j))
    return far + sorted(range(1, chips // 2), reverse=True)


def local(
    inputs,
    gate_values,
    write_proj,
    read_proj,
    step_raw,
    cotangent,
    step_bias,
    rate_log,
    skip_gain,
    norm_gain,
    state_bank,
    turn_index,
    turn_slot,
):
    devices = lax.axis_size("dp")
    chips = devices // 2
    slots, heads, hdim, dstate = state_bank.shape
    rows, _ = inputs.shape
    width = heads * hdim
    all_heads = devices * heads
    me = lax.axis_index("dp").astype(jnp.int32)
    me_array = me[None]

    def exchange(value, partner):
        return lax.ppermute(value, "dp", [(i, i ^ partner) for i in range(devices)])

    order = chip_order(chips)

    turn_values = turn_index.astype(BF16).reshape(rows // 128, 128)
    filler = jnp.zeros((TURN_ROWS - rows // 128, 128), BF16)
    packed_own = jnp.concatenate([read_proj, turn_values, filler], axis=0)
    packed = [packed_own] + [None] * (chips - 1)
    for j in order:
        packed[j] = exchange(packed_own, 2 * j)

    bank = state_bank.reshape(slots, width, dstate)
    lent = pick_states(me_array, turn_slot, bank)
    partner = exchange(lent, 1)
    begins, packed_all = start_reads(me_array, turn_slot, bank, partner, packed, rows, order + [0])
    packed_other = exchange(packed_all, 1)
    received = [begins[0]] + [None] * (chips - 1)
    for j in order:
        received[j] = exchange(begins[j], 2 * j)

    raw = step_raw.T.astype(F32) + step_bias[:, None]
    step = jax.nn.softplus(raw)
    pace = jnp.exp(rate_log)[:, None]
    rate = -pace * step
    position = jnp.arange(rows, dtype=jnp.int32)
    within = (position[:, None] <= position[None, :]) & (turn_index[:, None] == turn_index[None, :])
    within_f = within.astype(F32)
    inner = jnp.dot(rate, within_f, precision=HIGHEST)
    score = jnp.where(within, nt_dot(write_proj, read_proj), 0.0)
    inner_2 = inner * LOG2E
    inner_3 = inner_2.reshape(devices, heads, rows)
    source_3 = (inner_2 - jnp.log2(step)).reshape(devices, heads, rows)
    gain_row = norm_gain[None, :]

    previous = None
    back = {}
    for j in [0] + order:
        same, other, previous = mix(
            me_array,
            j,
            skip_gain,
            inputs,
            gate_values,
            cotangent,
            received[j],
            inner_3,
            source_3,
            gain_row,
            score,
            previous,
            heads,
            hdim,
        )
        back[2 * j] = same if j == 0 else exchange(same, 2 * j)
        back[2 * j + 1] = exchange(other, 2 * j + 1)
    grad_inputs, stats, gain_part = previous

    stats = stats.reshape(all_heads, 8, rows)
    d_rate = jnp.dot(stats[:, 0], within_f.T, precision=HIGHEST)
    d_step = stats[:, 1] / step - pace * d_rate
    head_part = jnp.stack(
        [
            jnp.sum(d_step * jax.nn.sigmoid(raw), axis=1),
            jnp.sum(d_rate * rate, axis=1),
            jnp.sum(stats[:, 2], axis=1),
        ]
    )
    gain_lines = gain_part[0].reshape(devices, width // 128, 128)
    head_count = 3 * all_heads
    head_lines = -(-head_count // 128)
    head_flat = jnp.pad(head_part.reshape(head_count), (0, head_lines * 128 - head_count))
    head_block = jnp.broadcast_to(head_flat.reshape(1, head_lines, 128), (devices, head_lines, 128))
    rest = jnp.zeros((devices, 8 - head_lines - width // 128, 128), F32)
    small = jnp.concatenate([gain_lines, head_block, rest], axis=1)
    small = jnp.sum(lax.all_to_all(small, "dp", split_axis=0, concat_axis=0, tiled=True), axis=0)
    gain_grad = small[: width // 128].reshape(width)
    head_grads = small[width // 128 : width // 128 + head_lines].reshape(-1)[:head_count].reshape(3, all_heads)

    sequence = [0, 1]
    for j in order:
        sequence += [2 * j, 2 * j + 1]
    cut = len(sequence) // 2
    state = None
    for part in (sequence[:cut], sequence[cut:]):
        state = state_grads(
            me_array,
            turn_slot,
            part,
            [back[q] for q in part],
            packed_all,
            packed_other,
            state,
            (slots, width, dstate),
        )
    return (grad_inputs, state.reshape(state_bank.shape), gain_grad, head_grads)


def solution(mesh):
    in_specs = (
        P(("groups", "dp"), None),
        P(("groups", "dp"), None),
        P(("groups", "dp"), None),
        P(("groups", "dp"), None),
        P(("groups", "dp"), None),
        P(("groups", "dp"), None),
        P(),
        P(),
        P(),
        P(),
        P("groups", "dp", None, None),
        P(("groups", "dp")),
        P("groups"),
    )
    out_specs = (
        P(("groups", "dp"), None),
        P("groups", "dp", None, None),
        P(("groups", "dp")),
        P("groups", None),
    )

    return jax.shard_map(local, mesh=mesh, in_specs=in_specs, out_specs=out_specs, check_vma=False)
```

time: 393 us -> 184 us (0.47)
  blocking collectives: 113 us -> 17.4 us
  matrix products: 90.7 us -> 1.64 us
  Pallas kernels: 0 us -> 65.6 us
  other arithmetic: 44.7 us -> 2.24 us
  local copies, waits for them, and re-layouts: 38.5 us -> 8.76 us
  between operations: 14.7 us -> 1.42 us
  waiting for transfers between devices: 60.7 us -> 51.2 us
  starting transfers between devices: 29 us -> 34.4 us
    all_gather x2 -> x0, blocking collectives: 113 us -> none  [the longest x1 63.3 us: local(): turns_all = lax.all_gather(turn_index, 'dp', axis=0, tiled=True)]
    dot_general x8 -> x3, matrix products: 90.7 us -> 1.64 us  [the longest x1 0.89 us: nt_dot(): lax.dot_general(a, b, (((1,), (1,)), ((), ())), preferred_element_type=F32)]
    pallas_call x0 -> x12, Pallas kernels: none -> 65.6 us  [the longest x8 44.3 us: mix(): pl.pallas_call(functools.partial(mix_kernel, chip_xor, heads, hdim, rows)...]
    all_to_all x5 -> x0, waiting for transfers between devices: 59.3 us -> none  [the longest x1 46.6 us: local(): lax.all_to_all(gate_values, 'dp', split_axis=1, concat_axis=0, tiled=True)]
    ppermute x0 -> x31, waiting for transfers between devices: none -> 51.2 us  [exchange(): return lax.ppermute(value, 'dp', [(i, i ^ partner) for i in range(devices)])]
    ppermute x0 -> x31, starting transfers between devices: none -> 34.4 us  [exchange(): return lax.ppermute(value, 'dp', [(i, i ^ partner) for i in range(devices)])]
    all_to_all x5 -> x0, starting transfers between devices: 28.9 us -> none  [the longest x1 6.9 us: local(): lax.all_to_all(inputs, 'dp', split_axis=1, concat_axis=0, tiled=True)]
    reduce_sum x7 -> x1, other arithmetic: 19.3 us -> 0.02 us  [local(): jnp.sum(lax.all_to_all(small, 'dp', split_axis=0, concat_axis=0, tiled=Tr...]
  transfers between devices with their start and end apart: 7 -> 31, of which waited for: 3 -> 13; matrix products, arithmetic and copies ran while one was open for 25% -> 4% of each run, Pallas kernels for 0% -> 27%
where the time goes in v1:
time: 184 us; the launch traced here: 183 us
  Pallas kernels  65.6 us (36%)
  waiting for transfers between devices  51.2 us (28%)
  starting transfers between devices  34.4 us (19%)
  blocking collectives  17.4 us (9%)
  local copies, waits for them, and re-layouts  8.76 us (5%)
  other arithmetic  2.24 us (1%)
    ppermute x31, waiting for transfers between devices, exchange(): return lax.ppermute(value, 'dp', [(i, i ^ partner) for i in range(devices)])  51.2 us
    pallas_call x8, Pallas kernels, mix(): pl.pallas_call(functools.partial(mix_kernel, chip_xor, heads, hdim, rows)...  44.3 us
    ppermute x31, starting transfers between devices, exchange(): return lax.ppermute(value, 'dp', [(i, i ^ partner) for i in range(devices)])  34.4 us
    all_to_all x1, blocking collectives, local(): lax.all_to_all(small, 'dp', split_axis=0, concat_axis=0, tiled=True)  17.4 us
    pallas_call x2, Pallas kernels, state_grads(): pl.pallas_call(functools.partial(state_kernel, partners, rows), out_shape...  10 us
    pallas_call x1, Pallas kernels, start_reads(): pl.pallas_call(functools.partial(start_kernel, chips, width, rows, order)...  7.32 us
    unnamed x100, local copies, waits for them, and re-layouts  5.1 us
    pallas_call x1, Pallas kernels, pick_states(): pl.pallas_call(functools.partial(bank_kernel, count), out_shape=jax.Shape...  3.96 us
  transfers between devices with their start and end apart: 31, of which 13 were waited for; matrix products, arithmetic and copies ran while one was open for 4% of the time, Pallas kernels for 27%

profile of v1, /device:TPU:9, one launch (start us, length us, event | category | flops | bytes accessed | tf_op | source)
XLA Modules:
  0.0 182.6 jit_solution(6510462992273168426)
XLA Ops:
  0.7 4.0 %pick_states.1 = bf16[32,256,128]{2,1,0:T(8,128)(2,1)} custom-call(s32[1]{0:T(128)} %bitcast.me_ref, s32[64]{0:T(128)} %slot_ref.7, bf16[64,256,128]{2,1,0:T(8,128)(2,1)} %bitcast.72), custom_call_target="tpu_custom_call" | custom-call | bytes 4194304 | tf_op jit(solution)/shard_map/pick_states/pallas_call | solution.py:57
  8.1 4.0 %collective-permute-start.5 = (bf16[272,128]{1,0:T(8,128)(2,1)S(1)}, bf16[272,128]{1,0:T(8,128)(2,1)S(1)}, u32[]{:S(2)}, u32[]{:S(2)}) collective-permute-start(bf16[272,128]{1,0:T(8,128)(2,1)S(1)} %maximum_maximum_fusion.refs_0_), channel_id=1, source_target_pairs={{0,10},{1,11},{2,8},{3,9},{4,14},{5,15},{6,12},{7,13},{8,2},{9,3},... | collective-permute-start | bytes 208904 | tf_op jit(solution)/shard_map/ppermute | solution.py:410
  13.4 3.1 %collective-permute-done.6.refs_6_ = bf16[272,128]{1,0:T(8,128)(2,1)S(1)} collective-permute-done((bf16[272,128]{1,0:T(8,128)(2,1)S(1)}, bf16[272,128]{1,0:T(8,128)(2,1)S(1)}, u32[]{:S(2)}, u32[]{:S(2)}) %collective-permute-start.6) | collective-permute-done | bytes 69664 | tf_op jit(solution)/shard_map/ppermute | solution.py:410
  23.5 7.3 %start_reads.1 = (bf16[512,256]{1,0:T(8,128)(2,1)}, bf16[512,256]{1,0:T(8,128)(2,1)}, bf16[512,256]{1,0:T(8,128)(2,1)}, bf16[512,256]{1,0:T(8,128)(2,1)}, bf16[5...) custom-call(s32[1]{0:T(128)} %bitcast.me_ref, ...), custom_call_target="tpu_custom_call" | custom-call | flops 1073741824 | bytes 6291456 | tf_op jit(solution)/shard_map/start_reads/pallas_call | solution.py:119
  30.9 4.1 %collective-permute-start.13 = (bf16[512,256]{1,0:T(8,128)(2,1)}, bf16[512,256]{1,0:T(8,128)(2,1)S(1)}, u32[]{:S(2)}, u32[]{:S(2)}) collective-permute-start(bf16[512,256]{1,0:T(8,128)(2,1)} %get-tuple-element.58), channel_id=1, source_target_pairs={{0,10},{1,11},{2,8},{3,9},{4,14},{5,15},{6,12},{7,13},{8,2},{9,3},... | collective-permute-start | bytes 786440 | tf_op jit(solution)/shard_map/ppermute | solution.py:410
  39.3 11.7 %collective-permute-done.13.begin_ref = bf16[512,256]{1,0:T(8,128)(2,1)S(1)} collective-permute-done((bf16[512,256]{1,0:T(8,128)(2,1)}, bf16[512,256]{1,0:T(8,128)(2,1)S(1)}, u32[]{:S(2)}, u32[]{:S(2)}) %collective-permute-start.13) | collective-permute-done | bytes 262176 | tf_op jit(solution)/shard_map/ppermute | solution.py:410
  52.6 4.1 %collective-permute-done.14.begin_ref = bf16[512,256]{1,0:T(8,128)(2,1)S(1)} collective-permute-done((bf16[512,256]{1,0:T(8,128)(2,1)}, bf16[512,256]{1,0:T(8,128)(2,1)S(1)}, u32[]{:S(2)}, u32[]{:S(2)}) %collective-permute-start.14) | collective-permute-done | bytes 262176 | tf_op jit(solution)/shard_map/ppermute | solution.py:410
  58.6 5.7 %mix.8 = (bf16[256,256]{1,0:T(8,128)(2,1)}, bf16[256,256]{1,0:T(8,128)(2,1)}, bf16[256,4096]{1,0:T(8,128)(2,1)}, f32[16,4,8,256]{3,2,1,0:T(8,128)}, f32[8,4096]{1,0:T(8,128)}) custom-call(s32[1]{0:T(128)} %bitcast.me_ref, f32[64]{0:T(128)} %skip_ref.15, bf16[256,4096]{1,0:T(8,128)(2,1)} %x_ref.15, bf16[256,4096]{1,0:T(8,128)(2,1)} %gate_ref.15, ...), custom_call_target="tpu_custom_call" | custom-call | flops 201326592 | bytes 1572864 | tf_op jit(solution)/shard_map/mix/pallas_call | solution.py:274
  64.4 5.5 %mix.9 = (bf16[256,256]{1,0:T(8,128)(2,1)}, bf16[256,256]{1,0:T(8,128)(2,1)}, bf16[256,4096]{1,0:T(8,128)(2,1)}, f32[16,4,8,256]{3,2,1,0:T(8,128)}, f32[8,4096]{1,0:T(8,128)}) custom-call(s32[1]{0:T(128)} %bitcast.me_ref, f32[64]{0:T(128)} %skip_ref.15, bf16[256,4096]{1,0:T(8,128)(2,1)} %x_ref.15, ...), custom_call_target="tpu_custom_call", output_to_operand_aliasing={{2}: (10, {}), {3}: (11, {}), {4}: (12, {})} | custom-call | flops 201326592 | bytes 1572864 | tf_op jit(solution)/shard_map/mix/pallas_call | solution.py:274
  69.9 5.5 %mix.10 = (bf16[256,256]{1,0:T(8,128)(2,1)}, bf16[256,256]{1,0:T(8,128)(2,1)}, bf16[256,4096]{1,0:T(8,128)(2,1)}, f32[16,4,8,256]{3,2,1,0:T(8,128)}, f32[8,4096]{1,0:T(8,128)}) custom-call(s32[1]{0:T(128)} %bitcast.me_ref, f32[64]{0:T(128)} %skip_ref.15, bf16[256,4096]{1,0:T(8,128)(2,1)} %x_ref.15, ...), custom_call_target="tpu_custom_call", output_to_operand_aliasing={{2}: (10, {}), {3}: (11, {}), {4}: (12, {})} | custom-call | flops 201326592 | bytes 1572864 | tf_op jit(solution)/shard_map/mix/pallas_call | solution.py:274
  75.4 5.4 %collective-permute-done.12.begin_ref = bf16[512,256]{1,0:T(8,128)(2,1)S(1)} collective-permute-done((bf16[512,256]{1,0:T(8,128)(2,1)}, bf16[512,256]{1,0:T(8,128)(2,1)S(1)}, u32[]{:S(2)}, u32[]{:S(2)}) %collective-permute-start.12) | collective-permute-done | bytes 262176 | tf_op jit(solution)/shard_map/ppermute | solution.py:410
  81.5 5.5 %mix.11 = (bf16[256,256]{1,0:T(8,128)(2,1)}, bf16[256,256]{1,0:T(8,128)(2,1)}, bf16[256,4096]{1,0:T(8,128)(2,1)}, f32[16,4,8,256]{3,2,1,0:T(8,128)}, f32[8,4096]{1,0:T(8,128)}) custom-call(s32[1]{0:T(128)} %bitcast.me_ref, f32[64]{0:T(128)} %skip_ref.15, bf16[256,4096]{1,0:T(8,128)(2,1)} %x_ref.15, ...), custom_call_target="tpu_custom_call", output_to_operand_aliasing={{2}: (10, {}), {3}: (11, {}), {4}: (12, {})} | custom-call | flops 201326592 | bytes 1572864 | tf_op jit(solution)/shard_map/mix/pallas_call | solution.py:274
  87.7 5.5 %mix.12 = (bf16[256,256]{1,0:T(8,128)(2,1)}, bf16[256,256]{1,0:T(8,128)(2,1)}, bf16[256,4096]{1,0:T(8,128)(2,1)}, f32[16,4,8,256]{3,2,1,0:T(8,128)}, f32[8,4096]{1,0:T(8,128)}) custom-call(s32[1]{0:T(128)} %bitcast.me_ref, f32[64]{0:T(128)} %skip_ref.15, bf16[256,4096]{1,0:T(8,128)(2,1)} %x_ref.15, ...), custom_call_target="tpu_custom_call", output_to_operand_aliasing={{2}: (10, {}), {3}: (11, {}), {4}: (12, {})} | custom-call | flops 201326592 | bytes 1572864 | tf_op jit(solution)/shard_map/mix/pallas_call | solution.py:274
  93.9 5.5 %mix.13 = (bf16[256,256]{1,0:T(8,128)(2,1)}, bf16[256,256]{1,0:T(8,128)(2,1)}, bf16[256,4096]{1,0:T(8,128)(2,1)}, f32[16,4,8,256]{3,2,1,0:T(8,128)}, f32[8,4096]{1,0:T(8,128)}) custom-call(s32[1]{0:T(128)} %bitcast.me_ref, f32[64]{0:T(128)} %skip_ref.15, bf16[256,4096]{1,0:T(8,128)(2,1)} %x_ref.15, ...), custom_call_target="tpu_custom_call", output_to_operand_aliasing={{2}: (10, {}), {3}: (11, {}), {4}: (12, {})} | custom-call | flops 201326592 | bytes 1572864 | tf_op jit(solution)/shard_map/mix/pallas_call | solution.py:274
  100.1 5.5 %mix.14 = (bf16[256,256]{1,0:T(8,128)(2,1)}, bf16[256,256]{1,0:T(8,128)(2,1)}, bf16[256,4096]{1,0:T(8,128)(2,1)}, f32[16,4,8,256]{3,2,1,0:T(8,128)}, f32[8,4096]{1,0:T(8,128)}) custom-call(s32[1]{0:T(128)} %bitcast.me_ref, f32[64]{0:T(128)} %skip_ref.15, bf16[256,4096]{1,0:T(8,128)(2,1)} %x_ref.15, ...), custom_call_target="tpu_custom_call", output_to_operand_aliasing={{2}: (10, {}), {3}: (11, {}), {4}: (12, {})} | custom-call | flops 201326592 | bytes 1572864 | tf_op jit(solution)/shard_map/mix/pallas_call | solution.py:274
  106.4 5.6 %mix.15 = (bf16[256,256]{1,0:T(8,128)(2,1)}, bf16[256,256]{1,0:T(8,128)(2,1)}, bf16[256,4096]{1,0:T(8,128)(2,1)}, f32[16,4,8,256]{3,2,1,0:T(8,128)}, f32[8,4096]{1,0:T(8,128)}) custom-call(s32[1]{0:T(128)} %bitcast.me_ref, f32[64]{0:T(128)} %skip_ref.15, bf16[256,4096]{1,0:T(8,128)(2,1)} %x_ref.15, ...), custom_call_target="tpu_custom_call", output_to_operand_aliasing={{2}: (10, {}), {3}: (11, {}), {4}: (12, {})} | custom-call | flops 201326592 | bytes 1572864 | tf_op jit(solution)/shard_map/mix/pallas_call | solution.py:274
  118.9 2.5 %collective-permute-start.30 = (bf16[256,256]{1,0:T(8,128)(2,1)S(1)}, bf16[256,256]{1,0:T(8,128)(2,1)S(1)}, u32[]{:S(2)}, u32[]{:S(2)}) collective-permute-start(bf16[256,256]{1,0:T(8,128)(2,1)S(1)} %copy-done.42), channel_id=1, source_target_pairs={{0,13},{1,12},{2,15},{3,14},{4,9},{5,8},{6,11},{7,10},{8,5},{9,4},... | collective-permute-start | bytes 393224 | tf_op jit(solution)/shard_map/ppermute | solution.py:410
  125.8 7.5 %collective-permute-done.29.refs_6_ = bf16[256,256]{1,0:T(8,128)(2,1)S(1)} collective-permute-done((bf16[256,256]{1,0:T(8,128)(2,1)S(1)}, bf16[256,256]{1,0:T(8,128)(2,1)S(1)}, u32[]{:S(2)}, u32[]{:S(2)}) %collective-permute-start.29) | collective-permute-done | bytes 131104 | tf_op jit(solution)/shard_map/ppermute | solution.py:410
  133.3 4.2 %collective-permute-done.30.refs_7_ = bf16[256,256]{1,0:T(8,128)(2,1)S(1)} collective-permute-done((bf16[256,256]{1,0:T(8,128)(2,1)S(1)}, bf16[256,256]{1,0:T(8,128)(2,1)S(1)}, u32[]{:S(2)}, u32[]{:S(2)}) %collective-permute-start.30) | collective-permute-done | bytes 131104 | tf_op jit(solution)/shard_map/ppermute | solution.py:410
  137.7 17.4 %all_to_all.5 = f32[16,8,128]{2,1,0:T(8,128)S(1)} all-to-all(f32[16,8,128]{2,1,0:T(8,128)S(1)} %maximum_maximum_fusion.1), channel_id=1, replica_groups=mesh['groups'=2,'dp'=16] {'dp'}, dimensions={0} | all-to-all | bytes 131072 | tf_op jit(solution)/shard_map/all_to_all | solution.py:484
  163.3 5.0 %state_grads.2.refs_8_ = bf16[64,256,128]{2,1,0:T(8,128)(2,1)} custom-call(s32[1]{0:T(128)} %bitcast.me_ref, s32[64]{0:T(128)} %slot_ref.7, bf16[8,272,128]{2,1,0:T(8,128)(2,1)} %get-tuple-element.83.same_ref, bf16[8,272,128]{2,1,0:T(8,128)(2,1)} %copy-done.2, bf16[256,256]{1,0:T(8,128)(2,1)} %get-tuple-element.92.refs_0_, bf16[256,256]{1,0:T(8,128)(2,1)} %copy-done.20, ...), custom_call_target="tpu_custom_call" | custom-call | flops 536870912 | bytes 4194304 | tf_op jit(solution)/shard_map/state_grads/pallas_call | solution.py:357
  168.4 2.6 %collective-permute-done.19.refs_3_ = bf16[256,256]{1,0:T(8,128)(2,1)S(1)} collective-permute-done((bf16[256,256]{1,0:T(8,128)(2,1)S(1)}, bf16[256,256]{1,0:T(8,128)(2,1)S(1)}, u32[]{:S(2)}, u32[]{:S(2)}) %collective-permute-start.19) | collective-permute-done | bytes 131104 | tf_op jit(solution)/shard_map/ppermute | solution.py:410
  171.0 5.8 %collective-permute-done.17.refs_1_ = bf16[256,256]{1,0:T(8,128)(2,1)S(1)} collective-permute-done((bf16[256,256]{1,0:T(8,128)(2,1)S(1)}, bf16[256,256]{1,0:T(8,128)(2,1)S(1)}, u32[]{:S(2)}, u32[]{:S(2)}) %collective-permute-start.17) | collective-permute-done | bytes 131104 | tf_op jit(solution)/shard_map/ppermute | solution.py:410
  177.4 5.0 %state_grads.3 = bf16[64,256,128]{2,1,0:T(8,128)(2,1)} custom-call(s32[1]{0:T(128)} %bitcast.me_ref, s32[64]{0:T(128)} %slot_ref.7, bf16[8,272,128]{2,1,0:T(8,128)(2,1)} %get-tuple-element.83.same_ref, bf16[8,272,128]{2,1,0:T(8,128)(2,1)} %copy-done.2, bf16[256,256]{1,0:T(8,128)(2,1)} %copy-done.18, ...), custom_call_target="tpu_custom_call", output_to_operand_aliasing={{}: (12, {})} | custom-call | flops 536870912 | bytes 4194304 | tf_op jit(solution)/shard_map/state_grads/pallas_call | solution.py:357
  (173 shorter events, 43.2 us)
Async XLA Ops:
  4.6 16.9 %collective-permute-start = (bf16[32,256,128]{2,1,0:T(8,128)(2,1)}, bf16[32,256,128]{2,1,0:T(8,128)(2,1)S(1)}, u32[]{:S(2)}, u32[]{:S(2)}) collective-permute-start(bf16[32,256,128]{2,1,0:T(8,128)(2,1)} %pick_states.1), channel_id=1, source_target_pairs={{0,1},{1,0},{2,3},{3,2},{4,5},{5,4},{6,7},{7,6},{8,9},{9,8},{10,11... | collective-permute-start | bytes 6291464 | tf_op jit(solution)/shard_map/ppermute | solution.py:410
  7.9 8.5 %collective-permute-start.6 = (bf16[272,128]{1,0:T(8,128)(2,1)S(1)}, bf16[272,128]{1,0:T(8,128)(2,1)S(1)}, u32[]{:S(2)}, u32[]{:S(2)}) collective-permute-start(bf16[272,128]{1,0:T(8,128)(2,1)S(1)} %maximum_maximum_fusion.refs_0_), channel_id=1, source_target_pairs={{0,12},{1,13},{2,14},{3,15},{4,8},{5,9},{6,10},{7,11},{8,4},{9,5},... | collective-permute-start | bytes 208904 | tf_op jit(solution)/shard_map/ppermute | solution.py:410
  8.1 10.3 %collective-permute-start.5 = (bf16[272,128]{1,0:T(8,128)(2,1)S(1)}, bf16[272,128]{1,0:T(8,128)(2,1)S(1)}, u32[]{:S(2)}, u32[]{:S(2)}) collective-permute-start(bf16[272,128]{1,0:T(8,128)(2,1)S(1)} %maximum_maximum_fusion.refs_0_), channel_id=1, source_target_pairs={{0,10},{1,11},{2,8},{3,9},{4,14},{5,15},{6,12},{7,13},{8,2},{9,3},... | collective-permute-start | bytes 208904 | tf_op jit(solution)/shard_map/ppermute | solution.py:410
  12.2 7.8 %collective-permute-start.4 = (bf16[272,128]{1,0:T(8,128)(2,1)S(1)}, bf16[272,128]{1,0:T(8,128)(2,1)S(1)}, u32[]{:S(2)}, u32[]{:S(2)}) collective-permute-start(bf16[272,128]{1,0:T(8,128)(2,1)S(1)} %maximum_maximum_fusion.refs_0_), channel_id=1, source_target_pairs={{0,8},{1,9},{2,10},{3,11},{4,12},{5,13},{6,14},{7,15},{8,0},{9,1},... | collective-permute-start | bytes 208904 | tf_op jit(solution)/shard_map/ppermute | solution.py:410
  30.9 20.1 %collective-permute-start.13 = (bf16[512,256]{1,0:T(8,128)(2,1)}, bf16[512,256]{1,0:T(8,128)(2,1)S(1)}, u32[]{:S(2)}, u32[]{:S(2)}) collective-permute-start(bf16[512,256]{1,0:T(8,128)(2,1)} %get-tuple-element.58), channel_id=1, source_target_pairs={{0,10},{1,11},{2,8},{3,9},{4,14},{5,15},{6,12},{7,13},{8,2},{9,3},... | collective-permute-start | bytes 786440 | tf_op jit(solution)/shard_map/ppermute | solution.py:410
  34.9 21.7 %collective-permute-start.14 = (bf16[512,256]{1,0:T(8,128)(2,1)}, bf16[512,256]{1,0:T(8,128)(2,1)S(1)}, u32[]{:S(2)}, u32[]{:S(2)}) collective-permute-start(bf16[512,256]{1,0:T(8,128)(2,1)} %get-tuple-element.59), channel_id=1, source_target_pairs={{0,8},{1,9},{2,10},{3,11},{4,12},{5,13},{6,14},{7,15},{8,0},{9,1},... | collective-permute-start | bytes 786440 | tf_op jit(solution)/shard_map/ppermute | solution.py:410
  36.6 69.0 %collective-permute-start.8 = (bf16[512,256]{1,0:T(8,128)(2,1)}, bf16[512,256]{1,0:T(8,128)(2,1)S(1)}, u32[]{:S(2)}, u32[]{:S(2)}) collective-permute-start(bf16[512,256]{1,0:T(8,128)(2,1)} %get-tuple-element.53), channel_id=1, source_target_pairs={{0,2},{1,3},{2,0},{3,1},{4,6},{5,7},{6,4},{7,5},{8,10},{9,11},{10,... | collective-permute-start | bytes 786440 | tf_op jit(solution)/shard_map/ppermute | solution.py:410
  37.3 62.1 %collective-permute-start.9 = (bf16[512,256]{1,0:T(8,128)(2,1)}, bf16[512,256]{1,0:T(8,128)(2,1)S(1)}, u32[]{:S(2)}, u32[]{:S(2)}) collective-permute-start(bf16[512,256]{1,0:T(8,128)(2,1)} %get-tuple-element.54), channel_id=1, source_target_pairs={{0,4},{1,5},{2,6},{3,7},{4,0},{5,1},{6,2},{7,3},{8,12},{9,13},{10,... | collective-permute-start | bytes 786440 | tf_op jit(solution)/shard_map/ppermute | solution.py:410
  38.3 54.9 %collective-permute-start.10 = (bf16[512,256]{1,0:T(8,128)(2,1)}, bf16[512,256]{1,0:T(8,128)(2,1)S(1)}, u32[]{:S(2)}, u32[]{:S(2)}) collective-permute-start(bf16[512,256]{1,0:T(8,128)(2,1)} %get-tuple-element.55), channel_id=1, source_target_pairs={{0,6},{1,7},{2,4},{3,5},{4,2},{5,3},{6,0},{7,1},{8,14},{9,15},{10,... | collective-permute-start | bytes 786440 | tf_op jit(solution)/shard_map/ppermute | solution.py:410
  51.0 36.0 %collective-permute-start.11 = (bf16[512,256]{1,0:T(8,128)(2,1)}, bf16[512,256]{1,0:T(8,128)(2,1)S(1)}, u32[]{:S(2)}, u32[]{:S(2)}) collective-permute-start(bf16[512,256]{1,0:T(8,128)(2,1)} %get-tuple-element.56), channel_id=1, source_target_pairs={{0,14},{1,15},{2,12},{3,13},{4,10},{5,11},{6,8},{7,9},{8,6},{9,7},... | collective-permute-start | bytes 786440 | tf_op jit(solution)/shard_map/ppermute | solution.py:410
  56.6 24.2 %collective-permute-start.12 = (bf16[512,256]{1,0:T(8,128)(2,1)}, bf16[512,256]{1,0:T(8,128)(2,1)S(1)}, u32[]{:S(2)}, u32[]{:S(2)}) collective-permute-start(bf16[512,256]{1,0:T(8,128)(2,1)} %get-tuple-element.57), channel_id=1, source_target_pairs={{0,12},{1,13},{2,14},{3,15},{4,8},{5,9},{6,10},{7,11},{8,4},{9,5},... | collective-permute-start | bytes 786440 | tf_op jit(solution)/shard_map/ppermute | solution.py:410
  80.8 79.7 %collective-permute-start.15 = (bf16[8,272,128]{2,1,0:T(8,128)(2,1)S(1)}, bf16[8,272,128]{2,1,0:T(8,128)(2,1)S(1)}, u32[]{:S(2)}, u32[]{:S(2)}) collective-permute-start(bf16[8,272,128]{2,1,0:T(8,128)(2,1)S(1)} %copy-done.1), channel_id=1, source_target_pairs={{0,1},{1,0},{2,3},{3,2},{4,5},{5,4},{6,7},{7,6},{8,9},{9,8},{10,11... | collective-permute-start | bytes 1671176 | tf_op jit(solution)/shard_map/ppermute | solution.py:410
  87.0 29.6 %collective-permute-start.24 = (bf16[256,256]{1,0:T(8,128)(2,1)S(1)}, bf16[256,256]{1,0:T(8,128)(2,1)S(1)}, u32[]{:S(2)}, u32[]{:S(2)}) collective-permute-start(bf16[256,256]{1,0:T(8,128)(2,1)S(1)} %copy-done.44), channel_id=1, source_target_pairs={{0,1},{1,0},{2,3},{3,2},{4,5},{5,4},{6,7},{7,6},{8,9},{9,8},{10,11... | collective-permute-start | bytes 393224 | tf_op jit(solution)/shard_map/ppermute | solution.py:410
  116.7 16.6 %collective-permute-start.29 = (bf16[256,256]{1,0:T(8,128)(2,1)S(1)}, bf16[256,256]{1,0:T(8,128)(2,1)S(1)}, u32[]{:S(2)}, u32[]{:S(2)}) collective-permute-start(bf16[256,256]{1,0:T(8,128)(2,1)S(1)} %copy-done.43), channel_id=1, source_target_pairs={{0,12},{1,13},{2,14},{3,15},{4,8},{5,9},{6,10},{7,11},{8,4},{9,5},... | collective-permute-start | bytes 393224 | tf_op jit(solution)/shard_map/ppermute | solution.py:410
  118.9 18.7 %collective-permute-start.30 = (bf16[256,256]{1,0:T(8,128)(2,1)S(1)}, bf16[256,256]{1,0:T(8,128)(2,1)S(1)}, u32[]{:S(2)}, u32[]{:S(2)}) collective-permute-start(bf16[256,256]{1,0:T(8,128)(2,1)S(1)} %copy-done.42), channel_id=1, source_target_pairs={{0,13},{1,12},{2,15},{3,14},{4,9},{5,8},{6,11},{7,10},{8,5},{9,4},... | collective-permute-start | bytes 393224 | tf_op jit(solution)/shard_map/ppermute | solution.py:410
  122.6 32.4 %collective-permute-start.27 = (bf16[256,256]{1,0:T(8,128)(2,1)}, bf16[256,256]{1,0:T(8,128)(2,1)S(1)}, u32[]{:S(2)}, u32[]{:S(2)}) collective-permute-start(bf16[256,256]{1,0:T(8,128)(2,1)} %get-tuple-element.96), channel_id=1, source_target_pairs={{0,10},{1,11},{2,8},{3,9},{4,14},{5,15},{6,12},{7,13},{8,2},{9,3},... | collective-permute-start | bytes 393224 | tf_op jit(solution)/shard_map/ppermute | solution.py:410
  123.9 32.6 %collective-permute-start.28 = (bf16[256,256]{1,0:T(8,128)(2,1)S(1)}, bf16[256,256]{1,0:T(8,128)(2,1)S(1)}, u32[]{:S(2)}, u32[]{:S(2)}) collective-permute-start(bf16[256,256]{1,0:T(8,128)(2,1)S(1)} %copy-done.41), channel_id=1, source_target_pairs={{0,11},{1,10},{2,9},{3,8},{4,15},{5,14},{6,13},{7,12},{8,3},{9,2},... | collective-permute-start | bytes 393224 | tf_op jit(solution)/shard_map/ppermute | solution.py:410
  133.3 23.9 %collective-permute-start.25 = (bf16[256,256]{1,0:T(8,128)(2,1)S(1)}, bf16[256,256]{1,0:T(8,128)(2,1)S(1)}, u32[]{:S(2)}, u32[]{:S(2)}) collective-permute-start(bf16[256,256]{1,0:T(8,128)(2,1)S(1)} %copy-done.38), channel_id=1, source_target_pairs={{0,8},{1,9},{2,10},{3,11},{4,12},{5,13},{6,14},{7,15},{8,0},{9,1},... | collective-permute-start | bytes 393224 | tf_op jit(solution)/shard_map/ppermute | solution.py:410
  137.6 21.6 %collective-permute-start.26 = (bf16[256,256]{1,0:T(8,128)(2,1)S(1)}, bf16[256,256]{1,0:T(8,128)(2,1)S(1)}, u32[]{:S(2)}, u32[]{:S(2)}) collective-permute-start(bf16[256,256]{1,0:T(8,128)(2,1)S(1)} %copy-done.36), channel_id=1, source_target_pairs={{0,9},{1,8},{2,11},{3,10},{4,13},{5,12},{6,15},{7,14},{8,1},{9,0},... | collective-permute-start | bytes 393224 | tf_op jit(solution)/shard_map/ppermute | solution.py:410
  155.1 13.3 %collective-permute-start.21 = (bf16[256,256]{1,0:T(8,128)(2,1)}, bf16[256,256]{1,0:T(8,128)(2,1)S(1)}, u32[]{:S(2)}, u32[]{:S(2)}) collective-permute-start(bf16[256,256]{1,0:T(8,128)(2,1)} %get-tuple-element.89), channel_id=1, source_target_pairs={{0,5},{1,4},{2,7},{3,6},{4,1},{5,0},{6,3},{7,2},{8,13},{9,12},{10,... | collective-permute-start | bytes 393224 | tf_op jit(solution)/shard_map/ppermute | solution.py:410
  156.5 11.9 %collective-permute-start.18 = (bf16[256,256]{1,0:T(8,128)(2,1)S(1)}, bf16[256,256]{1,0:T(8,128)(2,1)S(1)}, u32[]{:S(2)}, u32[]{:S(2)}) collective-permute-start(bf16[256,256]{1,0:T(8,128)(2,1)S(1)} %copy-done.40), channel_id=1, source_target_pairs={{0,6},{1,7},{2,4},{3,5},{4,2},{5,3},{6,0},{7,1},{8,14},{9,15},{10,... | collective-permute-start | bytes 393224 | tf_op jit(solution)/shard_map/ppermute | solution.py:410
  157.3 13.7 %collective-permute-start.19 = (bf16[256,256]{1,0:T(8,128)(2,1)S(1)}, bf16[256,256]{1,0:T(8,128)(2,1)S(1)}, u32[]{:S(2)}, u32[]{:S(2)}) collective-permute-start(bf16[256,256]{1,0:T(8,128)(2,1)S(1)} %copy-done.39), channel_id=1, source_target_pairs={{0,7},{1,6},{2,5},{3,4},{4,3},{5,2},{6,1},{7,0},{8,15},{9,14},{10,... | collective-permute-start | bytes 393224 | tf_op jit(solution)/shard_map/ppermute | solution.py:410
  159.2 11.8 %collective-permute-start.16 = (bf16[256,256]{1,0:T(8,128)(2,1)S(1)}, bf16[256,256]{1,0:T(8,128)(2,1)S(1)}, u32[]{:S(2)}, u32[]{:S(2)}) collective-permute-start(bf16[256,256]{1,0:T(8,128)(2,1)S(1)} %copy-done.37), channel_id=1, source_target_pairs={{0,14},{1,15},{2,12},{3,13},{4,10},{5,11},{6,8},{7,9},{8,6},{9,7},... | collective-permute-start | bytes 393224 | tf_op jit(solution)/shard_map/ppermute | solution.py:410
  160.5 16.3 %collective-permute-start.17 = (bf16[256,256]{1,0:T(8,128)(2,1)S(1)}, bf16[256,256]{1,0:T(8,128)(2,1)S(1)}, u32[]{:S(2)}, u32[]{:S(2)}) collective-permute-start(bf16[256,256]{1,0:T(8,128)(2,1)S(1)} %copy-done.35), channel_id=1, source_target_pairs={{0,15},{1,14},{2,13},{3,12},{4,11},{5,10},{6,9},{7,8},{8,7},{9,6},... | collective-permute-start | bytes 393224 | tf_op jit(solution)/shard_map/ppermute | solution.py:410
  (57 other events, 893.1 us)
